TPU v7x, 512 devices: a whole 4x8x8 slice. The times are simulated.
512 devices in a mesh: row: 32 (over x, y), col: 16 (over z, core).
Axes of the slice: x: 4, y: 8, z: 8, core: 2. Of those that a mesh axis runs over, the one named last changes fastest.
Arguments:
- features: bfloat16 [131072, 128], P(('row', 'col')), may hold values from -6 to 6
- degree: int32 [131072], P(('row', 'col')), may hold values from 1 to 256
- weight: bfloat16 [128, 128], replicated, may hold values from -0.5 to 0.5
- bias: float32 [128], replicated, may hold values from -3 to 3
- cotangent: bfloat16 [131072, 128], P(('row', 'col')), may hold values from -8 to 8
- tile_rows: int32 [32, 16, 128], P('row', 'col'), may hold values from 0 to 31
- tile_cols: int32 [32, 16, 128], P('row', 'col'), may hold values from 0 to 63
- tile_count: int32 [32, 16, 1], P('row', 'col'), may hold values from 32 to 128, as said below
- tile_codes: int32 [32, 16, 128, 256], P('row', 'col'), may hold values from 0 to 4095
Outputs:
- hidden: bfloat16 [131072, 128], P(('row', 'col'))
- grad_features: bfloat16 [131072, 128], P(('row', 'col'))
- grad_weight: float32 [128, 128], replicated
- grad_bias: float32 [128], replicated
Inputs may be any that keep to these rules, and one draw needn't show every extreme that they name: Only the first tile_count slots of a block are live; on some block the count is exactly 128. `tile_rows`: A tile position may repeat within a block; repeated tiles add.
All inputs are finite; a program needn't handle non-finite values.
Results may differ from a plain program's by a relative error of at most 0.019.
Values may be sent and summed in bfloat16 or wider, within the bound.
A program may use at most 64 MiB of HBM per device.

v0:
```python
import math
import jax
import jax.numpy as jnp
from jax import lax
from jax.sharding import PartitionSpec as P

BLOCK = 16


def tile_mask(code_block, living):
    tile_side = code_block.shape[1] // 2
    row_code = code_block[:, :tile_side][:, :, None]
    col_code = code_block[:, tile_side:][:, None, :]
    hashed = (row_code * col_code + row_code + 3 * col_code) % 4093
    return ((hashed < 64) & living[:, None, None]).astype(jnp.bfloat16)


def accumulate(codes_dev, rows_dev, cols_dev, count_dev, source, out_tiles, backward):
    tile_side = source.shape[1]
    width_feat = source.shape[2]

    def block_step(block_id, summed):
        slot_start = block_id * BLOCK
        code_block = lax.dynamic_slice_in_dim(codes_dev, slot_start, BLOCK, 0)
        row_block = lax.dynamic_slice_in_dim(rows_dev, slot_start, BLOCK, 0)
        col_block = lax.dynamic_slice_in_dim(cols_dev, slot_start, BLOCK, 0)
        slot_ids = slot_start + jnp.arange(BLOCK, dtype=jnp.int32)
        target = col_block if backward else row_block
        anchor = row_block if backward else col_block
        living = slot_ids < count_dev
        keep = tile_mask(code_block, living)
        picked = jnp.take(source, anchor, axis=0)
        if backward:
            product = jnp.einsum("tij,tif->tjf", keep, picked, preferred_element_type=jnp.float32)
        else:
            product = jnp.einsum("tij,tjf->tif", keep, picked, preferred_element_type=jnp.float32)
        return summed.at[target].add(product)

    start_sum = jnp.zeros((out_tiles, tile_side, width_feat), jnp.float32)
    loop_count = codes_dev.shape[0] // BLOCK
    summed = lax.fori_loop(0, loop_count, block_step, start_sum)
    return summed.reshape(out_tiles * tile_side, width_feat)


def dense_part(aggregate, weight, bias, cotangent, inv_root):
    preact = jnp.dot(aggregate, weight, preferred_element_type=jnp.float32) + bias
    hidden = jax.nn.elu(preact).astype(jnp.bfloat16)
    elu_slope = jnp.where(preact > 0, 1.0, jnp.exp(jnp.minimum(preact, 0.0)))
    grad_pre = cotangent.astype(jnp.float32) * elu_slope
    grad_pre_b = grad_pre.astype(jnp.bfloat16)
    grad_weight = lax.dot_general(
        aggregate, grad_pre_b, (((0,), (0,)), ((), ())), preferred_element_type=jnp.float32
    )
    grad_bias = jnp.sum(grad_pre, axis=0)
    grad_agg = jnp.dot(grad_pre_b, weight.T, preferred_element_type=jnp.float32)
    grad_scaled = (inv_root * grad_agg).astype(jnp.bfloat16)
    return (hidden, grad_weight, grad_bias, grad_scaled)


def local(features, degree, weight, bias, cotangent, tile_rows, tile_cols, tile_count, tile_codes):
    codes_dev = tile_codes[0, 0]
    rows_dev = tile_rows[0, 0]
    cols_dev = tile_cols[0, 0]
    count_dev = tile_count[0, 0, 0]
    pieces = features.shape[0]
    width_feat = features.shape[1]
    tile_side = codes_dev.shape[1] // 2
    row_devs = lax.axis_size("row")
    col_devs = lax.axis_size("col")
    grad_scale = 1.0 / math.sqrt(pieces * row_devs * col_devs)
    row_tiles = pieces * col_devs // tile_side
    col_tiles = pieces * row_devs // tile_side
    inv_root = lax.rsqrt(degree.astype(jnp.float32))[:, None]
    scaled = (inv_root * features.astype(jnp.float32)).astype(jnp.bfloat16)
    column_feats = lax.all_gather(scaled, "row", axis=0, tiled=True).reshape(
        col_tiles, tile_side, width_feat
    )
    row_terms = accumulate(codes_dev, rows_dev, cols_dev, count_dev, column_feats, row_tiles, False)
    agg_sum = lax.psum_scatter(
        row_terms.astype(jnp.bfloat16), "col", scatter_dimension=0, tiled=True
    ).astype(jnp.float32)
    aggregate = (inv_root * agg_sum).astype(jnp.bfloat16)
    hidden, grad_weight, grad_bias, grad_scaled = dense_part(
        aggregate, weight, bias, cotangent, inv_root
    )
    grad_weight, grad_bias = lax.psum(
        (grad_weight * grad_scale, grad_bias * grad_scale), ("row", "col")
    )
    row_grads = lax.all_gather(grad_scaled, "col", axis=0, tiled=True)
    row_sources = row_grads.reshape(row_tiles, tile_side, width_feat)
    col_terms = accumulate(codes_dev, rows_dev, cols_dev, count_dev, row_sources, col_tiles, True)
    grad_sum = lax.psum_scatter(
        col_terms.astype(jnp.bfloat16), "row", scatter_dimension=0, tiled=True
    ).astype(jnp.float32)
    grad_features = (inv_root * grad_sum).astype(jnp.bfloat16)
    return (hidden, grad_features, grad_weight, grad_bias)


def solution(mesh):
    placed = (
        P(("row", "col"), None),
        P(("row", "col")),
        P(),
        P(),
        P(("row", "col"), None),
        P("row", "col", None),
        P("row", "col", None),
        P("row", "col", None),
        P("row", "col", None, None),
    )
    return jax.shard_map(
        local,
        mesh=mesh,
        in_specs=placed,
        out_specs=(P(("row", "col"), None), P(("row", "col"), None), P(), P()),
        check_vma=False,
    )
```

profile of v0, /device:TPU:1, one launch (start us, length us, event | category | flops | bytes accessed | tf_op | source)
XLA Modules:
  0.0 838.8 jit_solution(7499523494927583328)
XLA Ops:
  7.9 1.6 multiply_convert_fusion.2
  9.6 86.1 %all-gather.3.cloned.1.call-done = bf16[8192,128]{1,0:T(8,128)(2,1)} async-done(((bf16[256,128]{1,0:T(8,128)(2,1)}), bf16[8192,128]{1,0:T(8,128)(2,1)}) %all-gather.3.cloned.1.call-update) | async-done | bytes 2097168 | tf_op jit(solution)/shard_map/all_gather | solution.py:75
  96.0 66.9 %while.30 = (s32[]{:T(128)}, f32[32,128,128]{2,1,0:T(8,128)S(1)}, s32[128]{0:T(128)S(1)}, s32[128,256]{1,0:T(8,128)}, s32[]{:T(128)}, /*index=5*/s32[128]{0:T(12...) while((s32[]{:T(128)}, f32[32,128,128]{2,1,0:T(8,128)S(1)}, ...), condition=%wide.region_2.3_spmd, body=%wide.region_0.2_spmd.sunk | while | flops 70519992 | bytes 5837511 | solution.py:41
  96.8 0.7 broadcast_multiply_fusion.5
  97.5 3.0 gather_fusion
  100.5 2.2 fusion.60
  102.7 1.6 scatter_fusion
  105.9 3.0 gather_fusion
  108.9 2.2 fusion.60
  111.1 1.6 scatter_fusion
  113.5 0.7 broadcast_multiply_fusion.5
  114.2 3.0 gather_fusion
  117.3 2.2 fusion.60
  119.4 1.6 scatter_fusion
  121.9 0.7 broadcast_multiply_fusion.5
  122.6 3.0 gather_fusion
  125.6 2.2 fusion.60
  127.8 1.6 scatter_fusion
  130.3 0.7 broadcast_multiply_fusion.5
  131.0 3.0 gather_fusion
  134.0 2.2 fusion.60
  136.2 1.6 scatter_fusion
  139.3 3.0 gather_fusion
  142.4 2.2 fusion.60
  144.5 1.6 scatter_fusion
  147.0 0.7 broadcast_multiply_fusion.5
  147.7 3.0 gather_fusion
  150.7 2.2 fusion.60
  152.9 1.6 scatter_fusion
  156.1 3.0 gather_fusion
  159.1 2.2 fusion.60
  161.3 1.6 scatter_fusion
  162.9 1.1 convert_element_type.54
  164.1 61.1 %reduce-scatter.3.cloned.1.call-done = bf16[256,128]{1,0:T(8,128)(2,1)} async-done(((bf16[4096,128]{1,0:T(8,128)(2,1)}), bf16[256,128]{1,0:T(8,128)(2,1)}) %reduce-scatter.3.cloned.1.call-update) | async-done | bytes 65552 | tf_op jit(solution)/shard_map/reduce_scatter | solution.py:79
  225.2 1.8 fusion.46
  227.0 0.8 fusion.42
  227.9 43.0 %all-gather.5.cloned.1.call-done = bf16[4096,128]{1,0:T(8,128)(2,1)} async-done(((bf16[256,128]{1,0:T(8,128)(2,1)}), bf16[4096,128]{1,0:T(8,128)(2,1)}) %all-gather.5.cloned.1.call-update) | async-done | bytes 1048592 | tf_op jit(solution)/shard_map/all_gather | solution.py:89
  270.9 2.4 broadcast_in_dim.119
  273.4 63.9 %while.31 = (s32[]{:T(128)}, f32[64,128,128]{2,1,0:T(8,128)}, s32[128]{0:T(128)S(1)}, s32[128,256]{1,0:T(8,128)}, s32[]{:T(128)}, /*index=5*/s32[128]{0:T(128)S(...) while((s32[]{:T(128)}, f32[64,128,128]{2,1,0:T(8,128)}, ...), condition=%wide.region_6.7_spmd, body=%wide.region_4.6_spmd.sunk | while | flops 70519992 | bytes 5837511 | solution.py:41
  274.2 0.7 broadcast_multiply_fusion.6
  275.5 2.4 fusion.63
  278.0 3.4 scatter_fusion.1
  282.2 0.7 broadcast_multiply_fusion.6
  283.5 2.4 fusion.63
  286.0 3.4 scatter_fusion.1
  291.5 2.4 fusion.63
  293.9 3.4 scatter_fusion.1
  299.5 2.4 fusion.63
  301.9 3.4 scatter_fusion.1
  307.5 2.4 fusion.63
  309.9 3.4 scatter_fusion.1
  315.5 2.4 fusion.63
  317.9 3.4 scatter_fusion.1
  323.5 2.4 fusion.63
  325.9 3.4 scatter_fusion.1
  331.5 2.4 fusion.63
  333.9 3.4 scatter_fusion.1
  337.3 3.9 convert_element_type.62
  341.3 98.5 %psum.15 = f32[128]{0:T(128)} all-reduce(f32[128]{0:T(128)S(1)} %broadcast_multiply_fusion.2), channel_id=1, replica_groups=mesh['row'=32,'col'=16] {'row','col'}, use_global_device_ids=true, to_apply=%region_10.11 | all-reduce | flops 128 | bytes 1024 | tf_op jit(solution)/shard_map/psum | solution.py:86
  439.8 0.9 convolution_multiply_fusion.1
  440.7 117.3 %reduce-scatter.5.cloned.1.call-done = bf16[256,128]{1,0:T(8,128)(2,1)} async-done(((bf16[8192,128]{1,0:T(8,128)(2,1)}), bf16[256,128]{1,0:T(8,128)(2,1)}) %reduce-scatter.5.cloned.1.call-update) | async-done | bytes 65552 | tf_op jit(solution)/shard_map/reduce_scatter | solution.py:92
  558.0 1.6 multiply_convert_fusion
  559.6 271.2 %all-reduce.2.cloned.1.call-done = f32[128,128]{1,0:T(8,128)} async-done(((f32[128,128]{1,0:T(8,128)}), f32[128,128]{1,0:T(8,128)}) %all-reduce.2.cloned.1.call-update) | async-done | bytes 65552 | tf_op jit(solution)/shard_map/psum | solution.py:86
  830.8 1.5 copy.28
  (92 shorter events, 25.8 us)
Async XLA Ops:
  7.2 218.1 %copy-start = (bf16[128,128]{1,0:T(8,128)(2,1)S(1)}, bf16[128,128]{1,0:T(8,128)(2,1)}, u32[]{:S(2)}) copy-start(bf16[128,128]{1,0:T(8,128)(2,1)} %param.15) | copy-start | bytes 98308
  7.2 88.8 %copy-start.3 = (s32[1,1,128]{2,1,0:T(1,128)S(1)}, s32[1,1,128]{2,1,0:T(1,128)}, u32[]{:S(2)}) copy-start(s32[1,1,128]{2,1,0:T(1,128)} %param.19) | copy-start | bytes 1540
  7.2 88.8 %copy-start.2 = (s32[1,1,128]{2,1,0:T(1,128)S(1)}, s32[1,1,128]{2,1,0:T(1,128)}, u32[]{:S(2)}) copy-start(s32[1,1,128]{2,1,0:T(1,128)} %param.18) | copy-start | bytes 1540
  7.2 88.5 %all-gather.3.cloned.1.call-start = ((), (), s32[]{:S(2)}) async-start(), calls=%async_computation.2 | async-start | bytes 2162688 | tf_op jit(solution)/shard_map/all_gather | solution.py:75
  9.5 215.7 %reduce-scatter.3.cloned.1.call-start = ((), (), s32[]{:S(2)}) async-start(), calls=%async_computation.3 | async-start | bytes 1114112 | tf_op jit(solution)/shard_map/reduce_scatter | solution.py:79
  162.9 62.3 %copy-start.4 = (bf16[256,128]{1,0:T(8,128)(2,1)S(1)}, bf16[256,128]{1,0:T(8,128)(2,1)}, u32[]{:S(2)}) copy-start(bf16[256,128]{1,0:T(8,128)(2,1)} %param.17) | copy-start | bytes 196612
  162.9 62.3 %copy-start.6 = (f32[128]{0:T(128)S(1)}, f32[128]{0:T(128)}, u32[]{:S(2)}) copy-start(f32[128]{0:T(128)} %param.16) | copy-start | bytes 1540
  164.1 106.8 %all-gather.5.cloned.1.call-start = ((), (), s32[]{:S(2)}) async-start(), calls=%async_computation.4 | async-start | bytes 1114112 | tf_op jit(solution)/shard_map/all_gather | solution.py:89
  227.8 330.2 %reduce-scatter.5.cloned.1.call-start = ((), (), s32[]{:S(2)}) async-start(), calls=%async_computation.5 | async-start | bytes 2162688 | tf_op jit(solution)/shard_map/reduce_scatter | solution.py:92
  270.9 2.5 copy-start.1
  341.2 98.6 %copy-start.5 = (bf16[256,128]{1,0:T(8,128)(2,1)S(1)}, bf16[256,128]{1,0:T(8,128)(2,1)}, u32[]{:S(2)}) copy-start(bf16[256,128]{1,0:T(8,128)(2,1)} %reduce-scatter.3.cloned.1.call-done) | copy-start | bytes 196612
  341.2 489.6 %all-reduce.2.cloned.1.call-start = ((), (), s32[]{:S(2)}) async-start(), calls=%async_computation.6 | async-start | bytes 131072 | tf_op jit(solution)/shard_map/psum | solution.py:86
Sparse Core Ops, SparseCore 0:
  11.8 83.9 all-gather.2
  164.2 60.9 reduce-scatter.2
  227.9 42.9 all-gather.4
  341.3 216.6 reduce-scatter.4
  563.4 267.3 all-reduce.1
where the time goes:
time: 841 us; the launch traced here: 839 us
  waiting for transfers between devices  579 us (69%)
  blocking collectives  98.5 us (12%)
  other arithmetic  73.3 us (9%)
  matrix products  40.1 us (5%)
  local copies, waits for them, and re-layouts  33.5 us (4%)
  between operations  13.9 us (2%)
    psum x1, waiting for transfers between devices, local(): lax.psum((grad_weight * grad_scale, grad_bias * grad_scale), ('row', 'col'))  271 us
    reduce_scatter x1, waiting for transfers between devices, local(): lax.psum_scatter(col_terms.astype(jnp.bfloat16), 'row', scatter_dimension...  117 us
    psum x1, blocking collectives, local(): lax.psum((grad_weight * grad_scale, grad_bias * grad_scale), ('row', 'col'))  98.5 us
    all_gather x1, waiting for transfers between devices, local(): lax.all_gather(scaled, 'row', axis=0, tiled=True)  86.1 us
    reduce_scatter x1, waiting for transfers between devices, local(): lax.psum_scatter(row_terms.astype(jnp.bfloat16), 'col', scatter_dimension...  61.1 us
    all_gather x1, waiting for transfers between devices, local(): row_grads = lax.all_gather(grad_scaled, 'col', axis=0, tiled=True)  43 us
    scatter-add x16, other arithmetic, block_step(): return summed.at[target].add(product)  39.9 us
    gather x16, local copies, waits for them, and re-layouts, block_step(): picked = jnp.take(source, anchor, axis=0)  29.3 us
  transfers between devices with their start and end apart: 5, of which 5 were waited for; matrix products, arithmetic and copies ran while one was open for 0% of the time, Pallas kernels for 0%

commit v1 on v0

--- a/solution.py
+++ b/solution.py
@@ -86,7 +86,10 @@
     grad_weight, grad_bias = lax.psum(
         (grad_weight * grad_scale, grad_bias * grad_scale), ("row", "col")
     )
-    row_grads = lax.all_gather(grad_scaled, "col", axis=0, tiled=True)
+    block_next = jnp.stack(jax.lax.axis_size("col") * [grad_scaled])
+    row_grads = jnp.concatenate(
+        jax.lax.all_to_all(block_next, "col", split_axis=0, concat_axis=0), axis=0
+    )
     row_sources = row_grads.reshape(row_tiles, tile_side, width_feat)
     col_terms = accumulate(codes_dev, rows_dev, cols_dev, count_dev, row_sources, col_tiles, True)
     grad_sum = lax.psum_scatter(

time: 841 us -> 833 us (level)
  waiting for transfers between devices: 579 us -> 563 us
    all_gather x1 -> x0, waiting for transfers between devices: 43 us -> none  [local(): row_grads = lax.all_gather(grad_scaled, 'col', axis=0, tiled=True)]
    all_to_all x0 -> x1, waiting for transfers between devices: none -> 27.9 us  [local(): jax.lax.all_to_all(block_next, 'col', split_axis=0, concat_axis=0)]
where the time goes in v1:
time: 833 us; the launch traced here: 831 us
  waiting for transfers between devices  563 us (68%)
  blocking collectives  98.3 us (12%)
  other arithmetic  73.4 us (9%)
  matrix products  39.5 us (5%)
  local copies, waits for them, and re-layouts  34.6 us (4%)
  between operations  13.9 us (2%)
    psum x1, waiting for transfers between devices, local(): lax.psum((grad_weight * grad_scale, grad_bias * grad_scale), ('row', 'col'))  271 us
    reduce_scatter x1, waiting for transfers between devices, local(): lax.psum_scatter(col_terms.astype(jnp.bfloat16), 'row', scatter_dimension...  117 us
    psum x1, blocking collectives, local(): lax.psum((grad_weight * grad_scale, grad_bias * grad_scale), ('row', 'col'))  98.3 us
    all_gather x1, waiting for transfers between devices, local(): lax.all_gather(scaled, 'row', axis=0, tiled=True)  86.1 us
    reduce_scatter x1, waiting for transfers between devices, local(): lax.psum_scatter(row_terms.astype(jnp.bfloat16), 'col', scatter_dimension...  61.1 us
    scatter-add x16, other arithmetic, block_step(): return summed.at[target].add(product)  40 us
    gather x16, local copies, waits for them, and re-layouts, block_step(): picked = jnp.take(source, anchor, axis=0)  29.2 us
    all_to_all x1, waiting for transfers between devices, local(): jax.lax.all_to_all(block_next, 'col', split_axis=0, concat_axis=0)  27.9 us
  transfers between devices with their start and end apart: 5, of which 5 were waited for; matrix products, arithmetic and copies ran while one was open for 0% of the time, Pallas kernels for 0%

profile of v1, /device:TPU:1, one launch (start us, length us, event | category | flops | bytes accessed | tf_op | source)
XLA Modules:
  0.0 830.6 jit_solution(2668109526447979278)
XLA Ops:
  7.9 1.6 multiply_convert_fusion.2
  9.6 86.1 %all-gather.2.cloned.1.call-done = bf16[8192,128]{1,0:T(8,128)(2,1)} async-done(((bf16[256,128]{1,0:T(8,128)(2,1)}), bf16[8192,128]{1,0:T(8,128)(2,1)}) %all-gather.2.cloned.1.call-update) | async-done | bytes 2097168 | tf_op jit(solution)/shard_map/all_gather | solution.py:75
  96.0 66.9 %while.30 = (s32[]{:T(128)}, f32[32,128,128]{2,1,0:T(8,128)S(1)}, s32[128]{0:T(128)S(1)}, s32[128,256]{1,0:T(8,128)}, s32[]{:T(128)}, /*index=5*/s32[128]{0:T(12...) while((s32[]{:T(128)}, f32[32,128,128]{2,1,0:T(8,128)S(1)}, ...), condition=%wide.region_2.3_spmd, body=%wide.region_0.2_spmd.sunk | while | flops 70519992 | bytes 5837511 | solution.py:41
  96.8 0.7 broadcast_multiply_fusion.5
  97.5 3.0 gather_fusion
  100.5 2.2 fusion.60
  102.7 1.6 scatter_fusion
  105.9 3.0 gather_fusion
  108.9 2.2 fusion.60
  111.1 1.6 scatter_fusion
  113.5 0.7 broadcast_multiply_fusion.5
  114.2 3.0 gather_fusion
  117.2 2.2 fusion.60
  119.4 1.6 scatter_fusion
  121.9 0.7 broadcast_multiply_fusion.5
  122.6 3.0 gather_fusion
  125.6 2.2 fusion.60
  127.8 1.6 scatter_fusion
  130.2 0.7 broadcast_multiply_fusion.5
  130.9 3.0 gather_fusion
  134.0 2.2 fusion.60
  136.1 1.6 scatter_fusion
  139.3 3.0 gather_fusion
  142.3 2.2 fusion.60
  144.5 1.6 scatter_fusion
  147.7 3.0 gather_fusion
  150.7 2.2 fusion.60
  152.9 1.6 scatter_fusion
  155.3 0.7 broadcast_multiply_fusion.5
  156.0 3.0 gather_fusion
  159.0 2.2 fusion.60
  161.2 1.6 scatter_fusion
  162.9 1.1 convert_element_type.54
  164.0 61.1 %reduce-scatter.3.cloned.1.call-done = bf16[256,128]{1,0:T(8,128)(2,1)} async-done(((bf16[4096,128]{1,0:T(8,128)(2,1)}), bf16[256,128]{1,0:T(8,128)(2,1)}) %reduce-scatter.3.cloned.1.call-update) | async-done | bytes 65552 | tf_op jit(solution)/shard_map/reduce_scatter | solution.py:79
  225.2 1.8 fusion.46
  227.1 1.2 stack.2
  228.3 7.3 all-to-all-start
  235.6 27.9 %all-to-all-done = bf16[16,256,128]{2,1,0:T(8,128)(2,1)S(1)} async-done(((bf16[16,256,128]{2,1,0:T(8,128)(2,1)}), bf16[16,256,128]{2,1,0:T(8,128)(2,1)S(1)}, u32[]{:S(2)}, u32[]{:S(2)}) %all-to-all-start) | async-done | bytes 1048608 | tf_op jit(solution)/shard_map/all_to_all | solution.py:91
  263.6 2.5 broadcast_in_dim.119
  266.1 64.0 %while.31 = (s32[]{:T(128)}, f32[64,128,128]{2,1,0:T(8,128)}, s32[128]{0:T(128)S(1)}, s32[128,256]{1,0:T(8,128)}, s32[]{:T(128)}, /*index=5*/s32[128]{0:T(128)S(...) while((s32[]{:T(128)}, f32[64,128,128]{2,1,0:T(8,128)}, ...), condition=%wide.region_6.7_spmd, body=%wide.region_4.6_spmd.sunk | while | flops 70519992 | bytes 5837511 | solution.py:41
  268.2 2.4 fusion.63
  270.7 3.4 scatter_fusion.1
  274.9 0.7 broadcast_multiply_fusion.6
  276.3 2.4 fusion.63
  278.7 3.4 scatter_fusion.1
  284.2 2.4 fusion.63
  286.7 3.4 scatter_fusion.1
  292.2 2.4 fusion.63
  294.6 3.4 scatter_fusion.1
  300.2 2.4 fusion.63
  302.7 3.4 scatter_fusion.1
  308.2 2.4 fusion.63
  310.7 3.4 scatter_fusion.1
  316.3 2.4 fusion.63
  318.7 3.4 scatter_fusion.1
  324.3 2.4 fusion.63
  326.7 3.4 scatter_fusion.1
  330.1 3.9 convert_element_type.62
  334.0 98.3 %psum.15 = f32[128]{0:T(128)} all-reduce(f32[128]{0:T(128)S(1)} %broadcast_multiply_fusion.2), channel_id=1, replica_groups=mesh['row'=32,'col'=16] {'row','col'}, use_global_device_ids=true, to_apply=%region_10.11 | all-reduce | flops 128 | bytes 1024 | tf_op jit(solution)/shard_map/psum | solution.py:86
  432.3 0.9 convolution_multiply_fusion.1
  433.2 116.6 %reduce-scatter.5.cloned.1.call-done = bf16[256,128]{1,0:T(8,128)(2,1)} async-done(((bf16[8192,128]{1,0:T(8,128)(2,1)}), bf16[256,128]{1,0:T(8,128)(2,1)}) %reduce-scatter.5.cloned.1.call-update) | async-done | bytes 65552 | tf_op jit(solution)/shard_map/reduce_scatter | solution.py:95
  549.9 1.6 multiply_convert_fusion
  551.4 271.2 %all-reduce.2.cloned.1.call-done = f32[128,128]{1,0:T(8,128)} async-done(((f32[128,128]{1,0:T(8,128)}), f32[128,128]{1,0:T(8,128)}) %all-reduce.2.cloned.1.call-update) | async-done | bytes 65552 | tf_op jit(solution)/shard_map/psum | solution.py:86
  822.6 1.5 copy.28
  (90 shorter events, 26.7 us)
Async XLA Ops:
  7.2 218.0 %copy-start = (bf16[128,128]{1,0:T(8,128)(2,1)S(1)}, bf16[128,128]{1,0:T(8,128)(2,1)}, u32[]{:S(2)}) copy-start(bf16[128,128]{1,0:T(8,128)(2,1)} %param.15) | copy-start | bytes 98308
  7.2 88.8 %copy-start.2 = (s32[1,1,128]{2,1,0:T(1,128)S(1)}, s32[1,1,128]{2,1,0:T(1,128)}, u32[]{:S(2)}) copy-start(s32[1,1,128]{2,1,0:T(1,128)} %param.19) | copy-start | bytes 1540
  7.2 88.8 %copy-start.1 = (s32[1,1,128]{2,1,0:T(1,128)S(1)}, s32[1,1,128]{2,1,0:T(1,128)}, u32[]{:S(2)}) copy-start(s32[1,1,128]{2,1,0:T(1,128)} %param.18) | copy-start | bytes 1540
  7.2 88.5 %all-gather.2.cloned.1.call-start = ((), (), s32[]{:S(2)}) async-start(), calls=%async_computation.3 | async-start | bytes 2162688 | tf_op jit(solution)/shard_map/all_gather | solution.py:75
  9.5 215.6 %reduce-scatter.3.cloned.1.call-start = ((), (), s32[]{:S(2)}) async-start(), calls=%async_computation.4 | async-start | bytes 1114112 | tf_op jit(solution)/shard_map/reduce_scatter | solution.py:79
  162.8 62.3 %copy-start.3 = (bf16[256,128]{1,0:T(8,128)(2,1)S(1)}, bf16[256,128]{1,0:T(8,128)(2,1)}, u32[]{:S(2)}) copy-start(bf16[256,128]{1,0:T(8,128)(2,1)} %param.17) | copy-start | bytes 196612
  162.8 62.3 %copy-start.5 = (f32[128]{0:T(128)S(1)}, f32[128]{0:T(128)}, u32[]{:S(2)}) copy-start(f32[128]{0:T(128)} %param.16) | copy-start | bytes 1540
  228.3 35.3 %all-to-all-start = ((bf16[16,256,128]{2,1,0:T(8,128)(2,1)}), bf16[16,256,128]{2,1,0:T(8,128)(2,1)S(1)}, u32[]{:S(2)}, u32[]{:S(2)}) async-start(bf16[16,256,128]{2,1,0:T(8,128)(2,1)} %stack.2), calls=%async_computation.1 | async-start | bytes 2097152 | tf_op jit(solution)/shard_map/all_to_all | solution.py:91
  235.6 314.3 %reduce-scatter.5.cloned.1.call-start = ((), (), s32[]{:S(2)}) async-start(), calls=%async_computation.5 | async-start | bytes 2162688 | tf_op jit(solution)/shard_map/reduce_scatter | solution.py:95
  334.0 98.4 %copy-start.4 = (bf16[256,128]{1,0:T(8,128)(2,1)S(1)}, bf16[256,128]{1,0:T(8,128)(2,1)}, u32[]{:S(2)}) copy-start(bf16[256,128]{1,0:T(8,128)(2,1)} %reduce-scatter.3.cloned.1.call-done) | copy-start | bytes 196612
  334.0 488.6 %all-reduce.2.cloned.1.call-start = ((), (), s32[]{:S(2)}) async-start(), calls=%async_computation.6 | async-start | bytes 131072 | tf_op jit(solution)/shard_map/psum | solution.py:86
Sparse Core Ops, SparseCore 0:
  11.8 83.9 all-gather.1
  164.1 60.9 reduce-scatter.2
  334.1 215.7 reduce-scatter.4
  555.3 267.2 all-reduce.1
